TPU v7x, 32 devices: a whole 2x2x4 slice. The times are simulated.
32 devices in a mesh: grp: 2 (over x), seq: 16 (over z, y, core).
Axes of the slice: x: 2, y: 2, z: 4, core: 2. Of those that a mesh axis runs over, the one named last changes fastest.
Arguments:
- queries: bfloat16 [8192, 8192], P(('grp', 'seq')), parts along dimension 0, may hold values from -6 to 6
- keys_in: bfloat16 [8192, 8192], P(('grp', 'seq')), parts along dimension 0, may hold values from -0.375 to 0.375
- values_in: bfloat16 [8192, 8192], P(('grp', 'seq')), parts along dimension 0, may hold values from -6 to 6
- log_decay: bfloat16 [8192, 64], P(('grp', 'seq')), parts along dimension 0, may hold values from -2 to 0, as said below
- gate_logits: bfloat16 [8192, 8192], P(('grp', 'seq')), parts along dimension 0, may hold values from -6 to 6
- norm_gain: float32 [8192], replicated, may hold values from 0.1 to 1.9
- doc_lengths: int32 [16], P('grp'), parts along dimension 0, may hold values from 1 to 2048, 4096 in all
Outputs:
- attended: bfloat16 [8192, 8192], P(('grp', 'seq')), parts along dimension 0
- final_state: float32 [128, 128, 128], P(('grp', 'seq')), parts along dimension 0
There are 2 independent parts, one for each index of `grp`. A program takes and returns all parts, laid end to end along the dimension named above; an argument that names none is the same for every part. Nothing has to cross between parts.
Inputs may be any that keep to these rules, and one draw needn't show every extreme that they name: log_decay is negative. `doc_lengths`: the 8 lengths are positive and sum to 4096.
All inputs are finite; a program needn't handle non-finite values.
Results may differ from a plain program's by a relative error of at most 0.0049.
Values may be sent and summed in bfloat16 or wider, within the bound.
A program may use at most 320 MiB of HBM per device.

v0:
```python
import math
import jax
import jax.numpy as jnp
from jax import lax
from jax.sharding import PartitionSpec as P

HEADS = 64
HEAD_DIM = 128
SPAN = 256
EPS = 1e-05


def doc_index(doc_lengths, positions):
    doc_ends = jnp.cumsum(doc_lengths)
    return jnp.sum((positions[:, None] >= doc_ends[None, :]).astype(jnp.int32), axis=1)


def local_terms(query_blk, key_blk, value_blk, decay_blk, doc_blk, prior_doc):
    length = query_blk.shape[1]
    row_index = lax.broadcasted_iota(jnp.int32, (length, length), 0)
    col_index = lax.broadcasted_iota(jnp.int32, (length, length), 1)
    causal = row_index >= col_index
    cumulative = jnp.einsum(
        "ij,gjh->gih", causal.astype(jnp.float32), decay_blk, precision=lax.Precision.HIGHEST
    )
    allowed = causal[None] & (doc_blk[:, :, None] == doc_blk[:, None, :])
    cumul_heads = jnp.swapaxes(cumulative, 1, 2)
    spread_log = jnp.where(
        allowed[:, None], cumul_heads[:, :, :, None] - cumul_heads[:, :, None, :], 0.0
    )
    decay_grid = jnp.where(allowed[:, None], jnp.exp(spread_log), 0.0)
    scores = jnp.einsum("gihd,gjhd->ghij", query_blk, key_blk, preferred_element_type=jnp.float32)
    weights = (scores * decay_grid).astype(jnp.bfloat16)
    inside = jnp.einsum("ghij,gjhd->gihd", weights, value_blk, preferred_element_type=jnp.float32)
    carried = (doc_blk == prior_doc[:, None]).astype(jnp.float32)
    leading = carried[:, :, None] * jnp.exp(cumulative)
    closing_doc = (doc_blk == doc_blk[:, -1:]).astype(jnp.float32)
    key_weight = closing_doc[:, :, None] * jnp.exp(cumulative[:, -1:, :] - cumulative)
    weighted = (key_blk.astype(jnp.float32) * key_weight[..., None]).astype(jnp.bfloat16)
    update = jnp.einsum("gjhd,gjhe->ghde", weighted, value_blk, preferred_element_type=jnp.float32)
    factor = carried[:, -1:] * jnp.exp(cumulative[:, -1, :])
    return (inside, leading, factor, update)


def span_pass(query_rows, key_rows, value_rows, decay_rows, documents, before):
    spans = query_rows.shape[0]
    per_step = math.gcd(spans, max(1, 32 // query_rows.shape[2]))

    def blocked(array):
        return array.reshape((spans // per_step, per_step) + array.shape[1:])

    pieces = lax.map(
        lambda batch_item: local_terms(*batch_item),
        tuple(
            (
                blocked(array)
                for array in (query_rows, key_rows, value_rows, decay_rows, documents, before)
            )
        ),
    )
    return tuple((array.reshape((spans,) + array.shape[2:]) for array in pieces))


def join_states(first_pair, second_pair):
    return (
        first_pair[0] * second_pair[0],
        second_pair[0][..., None, None] * first_pair[1] + second_pair[1],
    )


def prefix_states(factor, update):
    running_factor, running_update = lax.associative_scan(join_states, (factor, update), axis=0)
    prior_factor = jnp.concatenate([jnp.ones_like(factor[:1]), running_factor[:-1]], axis=0)
    prior_update = jnp.concatenate([jnp.zeros_like(update[:1]), running_update[:-1]], axis=0)
    return (prior_factor, prior_update, running_factor[-1], running_update[-1])


def with_state(query_rows, inside, leading, states):
    across = jnp.einsum(
        "nihd,nhde->nihe", query_rows.astype(jnp.float32), states, precision=lax.Precision.HIGHEST
    )
    return inside + across * leading[..., None]


def shards(queries, keys_in, values_in, log_decay, gate_logits, norm_gain, doc_lengths):
    local_len = queries.shape[0]
    spans = local_len // SPAN
    positions = lax.axis_index("seq") * local_len + lax.iota(jnp.int32, local_len)
    documents = doc_index(doc_lengths, positions).reshape(spans, SPAN)
    before = doc_index(doc_lengths, positions - 1).reshape(spans, SPAN)[:, 0]
    span_shape = (spans, SPAN, HEADS, HEAD_DIM)
    query_rows = queries.reshape(span_shape)
    key_rows = keys_in.reshape(span_shape)
    value_rows = values_in.reshape(span_shape)
    decay_rows = log_decay.astype(jnp.float32).reshape(spans, SPAN, HEADS)
    inside, leading, factor, update = span_pass(
        query_rows, key_rows, value_rows, decay_rows, documents, before
    )
    prior_factor, prior_update, device_factor, device_update = prefix_states(factor, update)
    owner_factor, owner_update = (
        lax.all_to_all(
            device_factor.reshape(1, HEADS), "seq", split_axis=1, concat_axis=0, tiled=True
        ),
        lax.all_to_all(
            device_update.reshape(1, HEADS, HEAD_DIM, HEAD_DIM),
            "seq",
            split_axis=1,
            concat_axis=0,
            tiled=True,
        ),
    )
    entry_factor, entry_update, total_factor, total_update = prefix_states(
        owner_factor, owner_update
    )
    incoming_update = lax.all_to_all(
        entry_update, "seq", split_axis=0, concat_axis=1, tiled=True
    ).reshape(HEADS, HEAD_DIM, HEAD_DIM)
    states = prior_factor[:, :, None, None] * incoming_update[None] + prior_update
    mixed = with_state(query_rows, inside, leading, states).reshape(local_len, HEADS * HEAD_DIM)
    inverse_rms = lax.rsqrt(jnp.mean(mixed * mixed, axis=1, keepdims=True) + EPS)
    gated = (
        mixed * inverse_rms * norm_gain[None, :] * jax.nn.sigmoid(gate_logits.astype(jnp.float32))
    )
    return (gated.astype(jnp.bfloat16), total_update)


def solution(mesh):
    in_specs = (
        P(("grp", "seq"), None),
        P(("grp", "seq"), None),
        P(("grp", "seq"), None),
        P(("grp", "seq"), None),
        P(("grp", "seq"), None),
        P(),
        P("grp"),
    )
    out_specs = (P(("grp", "seq"), None), P(("grp", "seq"), None, None))
    return jax.shard_map(shards, mesh=mesh, in_specs=in_specs, out_specs=out_specs, check_vma=False)
```

profile of v0, /device:TPU:13, one launch (start us, length us, event | category | flops | bytes accessed | tf_op | source)
XLA Modules:
  0.0 327.3 jit_solution(16462266262842617301)
XLA Ops:
  0.7 0.8 reduce-window.8
  1.5 0.1 convert_reduce_fusion
  1.6 0.5 slice.150
  2.1 0.6 slice.147
  4.0 0.2 fusion.25
  4.1 0.2 multiply_reduce_fusion.1
  4.3 0.7 mul.191
  5.0 6.5 %all-to-all-start.1 = ((f32[1,16,4]{2,0,1:T(1,128)}), f32[1,16,4]{2,0,1:T(1,128)S(1)}, u32[]{:S(2)}, u32[]{:S(2)}) async-start(f32[1,16,4]{2,0,1:T(1,128)} %bitcast.18), calls=%async_computation.1 | async-start | bytes 16384 | tf_op jit(solution)/shard_map/all_to_all | solution.py:101
  11.6 6.4 %copy.65 = bf16[256,8192]{0,1:T(8,128)(2,1)} copy(bf16[256,8192]{1,0:T(8,128)(2,1)} %param.8) | data formatting | bytes 8388608 | tf_op jit(solution)/shard_map/reshape.12
  17.9 1.2 compare_convert_fusion.1
  19.2 0.1 multiply_bitcast_fusion.1
  19.3 6.7 %fusion.17 = f32[1,64,128,128]{3,2,0,1:T(8,128)} fusion(bf16[256,64,128]{0,2,1:T(8,128)(2,1)} %bitcast.85, f32[256,64]{0,1:T(8,128)S(1)} %get-tuple-element.32, bf16[256,8192]{1,0:T(8,128)(2,1)} %param.9), kind=kOutput, calls=%fused_computation.19 | convolution fusion | flops 543162368 | bytes 12648448 | tf_op jit(solution)/shard_map/while/body/eval_jaxpr/gjhd,gjhe->ghde/dot_general | solution.py:40
  26.0 6.0 %all-to-all-start = ((f32[1,64,128,128]{3,2,0,1:T(8,128)}), f32[1,64,128,128]{3,2,0,1:T(8,128)}, u32[]{:S(2)}, u32[]{:S(2)}) async-start(f32[1,64,128,128]{3,2,0,1:T(8,128)} %fusion.17), calls=%async_computation | async-start | bytes 8388608 | tf_op jit(solution)/shard_map/all_to_all | solution.py:104
  32.0 0.1 copy.56
  32.1 0.1 slice.120
  32.2 0.1 slice.124
  32.3 0.1 slice.119
  32.4 0.1 copy.58
  32.4 0.1 slice.126
  32.5 0.1 slice.130
  32.6 0.1 slice.125
  32.7 0.1 copy.60
  32.8 0.1 slice.132
  32.9 0.1 slice.136
  33.0 0.1 copy.57
  33.1 0.1 copy.59
  33.2 0.1 copy.61
  33.3 0.2 slice_reduce_fusion.2
  33.5 0.2 slice_reduce_fusion.1
  33.7 90.8 %all-to-all-done = f32[1,64,128,128]{3,2,0,1:T(8,128)} async-done(((f32[1,64,128,128]{3,2,0,1:T(8,128)}), f32[1,64,128,128]{3,2,0,1:T(8,128)}, u32[]{:S(2)}, u32[]{:S(2)}) %all-to-all-start) | async-done | bytes 4194336 | tf_op jit(solution)/shard_map/all_to_all | solution.py:104
  124.5 1.0 slice_bitcast_fusion
  125.4 2.5 slice_add_fusion.1
  127.9 0.7 slice.152
  128.7 0.2 slice_add_fusion.2
  128.8 0.1 slice_add_fusion.3
  128.9 0.1 slice_add_fusion.4
  129.0 0.8 pad_add_fusion
  129.9 0.1 fusion.28
  130.0 0.9 pad_maximum_fusion.2
  130.8 3.5 %pad.28 = f32[4,4,128,128]{3,2,1,0:T(8,128)S(1)} pad(f32[2,4,128,128]{3,2,1,0:T(8,128)} %pad_maximum_fusion.2, f32[]{:T(128)} %constant.28.clone.1), padding=0_1_1x0_0_0x0_0_0x0_0_0 | pad | bytes 1572868 | tf_op jit(solution)/shard_map/pad | solution.py:72
  134.3 5.8 %pad.29 = f32[4,4,128,128]{3,2,1,0:T(8,128)} pad(f32[2,4,128,128]{3,2,1,0:T(8,128)} %pad_add_fusion, f32[]{:T(128)} %constant.28.clone.1), padding=1_0_1x0_0_0x0_0_0x0_0_0 | pad | bytes 1572868 | tf_op jit(solution)/shard_map/pad | solution.py:72
  140.1 2.4 add.96
  142.5 1.3 fusion.21
  143.8 0.1 pad_maximum_fusion.1
  143.9 6.3 %pad.30 = f32[8,4,128,128]{3,2,1,0:T(8,128)} pad(f32[4,4,128,128]{3,2,1,0:T(8,128)S(1)} %pad_maximum_fusion.1, f32[]{:T(128)} %constant.28.clone.1), padding=0_1_1x0_0_0x0_0_0x0_0_0 | pad | bytes 3145732 | tf_op jit(solution)/shard_map/pad | solution.py:72
  150.2 6.4 %pad.31 = f32[8,4,128,128]{3,2,1,0:T(8,128)} pad(f32[4,4,128,128]{3,2,1,0:T(8,128)S(1)} %copy-done.4, f32[]{:T(128)} %constant.28.clone.1), padding=1_0_1x0_0_0x0_0_0x0_0_0 | pad | bytes 3145732 | tf_op jit(solution)/shard_map/pad | solution.py:72
  156.6 2.6 add.98
  159.2 0.2 copy-done.2
  159.4 0.6 copy-done.3
  160.1 1.8 fusion.20
  161.9 1.5 pad_maximum_fusion
  163.4 18.4 %pad.32 = f32[16,4,128,128]{3,2,1,0:T(8,128)} pad(f32[8,4,128,128]{3,2,1,0:T(8,128)} %pad_maximum_fusion, f32[]{:T(128)} %constant.28.clone.1), padding=0_1_1x0_0_0x0_0_0x0_0_0 | pad | bytes 6291460 | tf_op jit(solution)/shard_map/pad | solution.py:72
  181.8 12.0 %pad.33 = f32[16,4,128,128]{3,2,1,0:T(8,128)} pad(f32[8,4,128,128]{3,2,1,0:T(8,128)S(1)} %add.98, f32[]{:T(128)} %constant.28.clone.1), padding=1_0_1x0_0_0x0_0_0x0_0_0 | pad | bytes 6291460 | tf_op jit(solution)/shard_map/pad | solution.py:72
  193.8 4.0 %slice_add_fusion = f32[15,4,128,128]{3,2,1,0:T(8,128)S(1)} fusion(f32[16,4,128,128]{3,2,1,0:T(8,128)} %pad.33, f32[16,4,128,128]{3,2,1,0:T(8,128)} %pad.32), kind=kLoop, calls=%fused_computation.14 | loop fusion | flops 983040 | bytes 11796480 | tf_op jit(solution)/shard_map/add | solution.py:72
  197.8 2.5 concatenate.15
  200.2 4.9 %all-to-all-start.2 = ((f32[16,4,128,128]{3,2,1,0:T(8,128)}), f32[16,4,128,128]{3,2,1,0:T(8,128)}, u32[]{:S(2)}, u32[]{:S(2)}) async-start(f32[16,4,128,128]{3,2,1,0:T(8,128)} %concatenate.15), calls=%async_computation.2 | async-start | bytes 8388608 | tf_op jit(solution)/shard_map/all_to_all | solution.py:115
  205.1 0.1 fusion.26
  205.3 11.7 %fusion.2 = f32[64,256,128]{1,2,0:T(8,128)} fusion(bf16[256,64,128]{0,2,1:T(8,128)(2,1)} %bitcast.86, f32[64,256]{1,0:T(8,128)S(1)} %bitcast.88, pred[256,256]{1,0:T(8,128)(4,1)S(1)} %fusion.26, bf16[256,8192]{1,0:T(8,128)(2,1)} %param.9, bf16[256,8192]{1,0:T(8,128)(2,1)} %param.7), kind=kOutput, calls=%fused_computation.7 | convolution fusion | flops 2168455168 | bytes 21102592 | tf_op jit(solution)/shard_map/while/body/eval_jaxpr/ghij,gjhd->gihd/dot_general | solution.py:34
  217.0 12.0 %pad.62 = f32[15,4,128,128]{3,2,1,0:T(8,128)} pad(f32[8,4,128,128]{3,2,1,0:T(8,128)S(1)} %add.98, f32[]{:T(128)} %constant.28.clone.1), padding=0_0_1x0_0_0x0_0_0x0_0_0 | pad | bytes 6029316
  229.0 1.7 add_bitcast_fusion
  230.7 66.9 %all-to-all-done.2 = f32[16,4,128,128]{3,2,1,0:T(8,128)} async-done(((f32[16,4,128,128]{3,2,1,0:T(8,128)}), f32[16,4,128,128]{3,2,1,0:T(8,128)}, u32[]{:S(2)}, u32[]{:S(2)}) %all-to-all-start.2) | async-done | bytes 4194336 | tf_op jit(solution)/shard_map/all_to_all | solution.py:115
  297.6 13.6 %multiply_reduce_fusion = (f32[256]{0:T(256)S(1)}, f32[1,256,64,128]{1,3,2,0:T(8,128)}) fusion(f32[256,64]{0,1:T(8,128)S(1)} %get-tuple-element.44, f32[64,128,128]{2,1,0:T(8,128)} %bitcast.33, f32[64,256,128]{1,2,0:T(8,128)} %fusion.2, bf16[256,8192]{1,0:T(8,128)(2,1)} %param.7), kind=kOutput, calls=%fused_computation.4 | convolution fusion | flops 3229613824 | bytes 25232384 | tf_op jit(solution)/shard_map/nihd,nhde->nihe/dot_general | solution.py:79
  311.3 8.9 %copy.64 = f32[256,8192]{1,0:T(8,128)} copy(f32[256,8192]{0,1:T(8,128)} %bitcast.84) | data formatting | bytes 16777216 | tf_op jit(solution)/shard_map/reshape | solution.py:119
  320.2 7.2 %multiply_convert_fusion.1 = bf16[256,8192]{1,0:T(8,128)(2,1)} fusion(bf16[256,8192]{1,0:T(8,128)(2,1)} %param.11, f32[256,8192]{1,0:T(8,128)} %copy.64, f32[8192]{0:T(1024)S(1)} %copy-done.8, f32[256]{0:T(256)S(1)} %add_rsqrt_fusion), kind=kLoop, calls=%fused_computation.3 | loop fusion | flops 16777216 | bytes 16811008 | tf_op jit(solution)/shard_map/convert_element_type | solution.py:124
  (22 shorter events, 0.1 us)
Async XLA Ops:
  0.6 3.3 %copy-start = (bf16[256,64]{0,1:T(8,128)(2,1)S(1)}, bf16[256,64]{0,1:T(8,128)(2,1)}, u32[]{:S(2)}) copy-start(bf16[256,64]{0,1:T(8,128)(2,1)} %param.10) | copy-start | bytes 98308
  4.1 15.0 %copy-start.6 = (f32[256,64]{0,1:T(8,128)}, f32[256,64]{0,1:T(8,128)S(1)}, u32[]{:S(2)}) copy-start(f32[256,64]{0,1:T(8,128)S(1)} %fusion.25) | copy-start | bytes 196612
  5.0 20.9 %all-to-all-start.1 = ((f32[1,16,4]{2,0,1:T(1,128)}), f32[1,16,4]{2,0,1:T(1,128)S(1)}, u32[]{:S(2)}, u32[]{:S(2)}) async-start(f32[1,16,4]{2,0,1:T(1,128)} %bitcast.18), calls=%async_computation.1 | async-start | bytes 16384 | tf_op jit(solution)/shard_map/all_to_all | solution.py:101
  26.0 98.5 %all-to-all-start = ((f32[1,64,128,128]{3,2,0,1:T(8,128)}), f32[1,64,128,128]{3,2,0,1:T(8,128)}, u32[]{:S(2)}, u32[]{:S(2)}) async-start(f32[1,64,128,128]{3,2,0,1:T(8,128)} %fusion.17), calls=%async_computation | async-start | bytes 8388608 | tf_op jit(solution)/shard_map/all_to_all | solution.py:104
  140.1 3.7 %copy-start.5 = (f32[1,4,128,128]{3,2,1,0:T(8,128)S(1)}, f32[1,4,128,128]{3,2,1,0:T(8,128)}, u32[]{:S(2)}) copy-start(f32[1,4,128,128]{3,2,1,0:T(8,128)} %slice.152) | copy-start | bytes 786436
  143.8 6.4 %copy-start.4 = (f32[4,4,128,128]{3,2,1,0:T(8,128)S(1)}, f32[4,4,128,128]{3,2,1,0:T(8,128)}, u32[]{:S(2)}) copy-start(f32[4,4,128,128]{3,2,1,0:T(8,128)} %add.96) | copy-start | bytes 3145732
  156.6 2.9 copy-start.2
  156.6 3.5 %copy-start.3 = (f32[8,4,128,128]{3,2,1,0:T(8,128)S(1)}, f32[8,4,128,128]{3,2,1,0:T(8,128)}, u32[]{:S(2)}) copy-start(f32[8,4,128,128]{3,2,1,0:T(8,128)} %pad.31) | copy-start | bytes 6291460
  200.2 5.0 %copy-start.7 = (f32[256,64]{0,1:T(8,128)S(1)}, f32[256,64]{0,1:T(8,128)}, u32[]{:S(2)}) copy-start(f32[256,64]{0,1:T(8,128)} %copy-done.6) | copy-start | bytes 196612
  200.2 97.4 %all-to-all-start.2 = ((f32[16,4,128,128]{3,2,1,0:T(8,128)}), f32[16,4,128,128]{3,2,1,0:T(8,128)}, u32[]{:S(2)}, u32[]{:S(2)}) async-start(f32[16,4,128,128]{3,2,1,0:T(8,128)} %concatenate.15), calls=%async_computation.2 | async-start | bytes 8388608 | tf_op jit(solution)/shard_map/all_to_all | solution.py:115
  311.3 8.9 %copy-start.8 = (f32[8192]{0:T(1024)S(1)}, f32[8192]{0:T(1024)}, u32[]{:S(2)}) copy-start(f32[8192]{0:T(1024)} %param.12) | copy-start | bytes 98308
  320.2 7.2 %copy-start.1 = (bf16[256,64]{0,1:T(8,128)(2,1)S(1)}, bf16[256,64]{0,1:T(8,128)(2,1)}, u32[]{:S(2)}) copy-start(bf16[256,64]{0,1:T(8,128)(2,1)} %param.10) | copy-start | bytes 98308
where the time goes:
time: 330 us; the launch traced here: 327 us
  waiting for transfers between devices  158 us (48%)
  local copies, waits for them, and re-layouts  88.2 us (27%)
  matrix products  32.2 us (10%)
  other arithmetic  29.8 us (9%)
  starting transfers between devices  17.5 us (5%)
    all_to_all x1, waiting for transfers between devices, shards(): lax.all_to_all(device_update.reshape(1, HEADS, HEAD_DIM, HEAD_DIM), 'seq'...  90.8 us
    all_to_all x1, waiting for transfers between devices, shards(): lax.all_to_all(entry_update, 'seq', split_axis=0, concat_axis=1, tiled=True)  66.9 us
    pad x6, local copies, waits for them, and re-layouts, prefix_states(): lax.associative_scan(join_states, (factor, update), axis=0)  52.3 us
    dot_general x1, matrix products, with_state(): jnp.einsum('nihd,nhde->nihe', query_rows.astype(jnp.float32), states, pre...  13.6 us
    unnamed x19, local copies, waits for them, and re-layouts  12.9 us
    dot_general x1, matrix products, local_terms(): jnp.einsum('ghij,gjhd->gihd', weights, value_blk, preferred_element_type=...  11.7 us
    add x4, other arithmetic, prefix_states(): lax.associative_scan(join_states, (factor, update), axis=0)  9.85 us
    reshape x1, local copies, waits for them, and re-layouts, shards(): with_state(query_rows, inside, leading, states)  8.91 us
  transfers between devices with their start and end apart: 3, of which 2 were waited for; matrix products, arithmetic and copies ran while one was open for 13% of the time, Pallas kernels for 0%

commit v1 on v0

--- a/solution.py
+++ b/solution.py
@@ -83,6 +83,14 @@
 
 
 def shards(queries, keys_in, values_in, log_decay, gate_logits, norm_gain, doc_lengths):
+
+    def supply_map(local_values):
+        h_now = jax.lax.axis_size("seq")
+        local_part = jnp.split(local_values, h_now, 0)
+        fresh = jnp.stack(local_part, 0)
+        row_out = jax.lax.all_to_all(fresh, "seq", 0, 0)
+        return jnp.concatenate(row_out, 1)
+
     local_len = queries.shape[0]
     spans = local_len // SPAN
     positions = lax.axis_index("seq") * local_len + lax.iota(jnp.int32, local_len)
@@ -112,9 +120,7 @@
     entry_factor, entry_update, total_factor, total_update = prefix_states(
         owner_factor, owner_update
     )
-    incoming_update = lax.all_to_all(
-        entry_update, "seq", split_axis=0, concat_axis=1, tiled=True
-    ).reshape(HEADS, HEAD_DIM, HEAD_DIM)
+    incoming_update = supply_map(entry_update).reshape(HEADS, HEAD_DIM, HEAD_DIM)
     states = prior_factor[:, :, None, None] * incoming_update[None] + prior_update
     mixed = with_state(query_rows, inside, leading, states).reshape(local_len, HEADS * HEAD_DIM)
     inverse_rms = lax.rsqrt(jnp.mean(mixed * mixed, axis=1, keepdims=True) + EPS)

time: 330 us -> 353 us (1.070)
  other arithmetic: 29.8 us -> 51.6 us
    unnamed x0 -> x14, other arithmetic: none -> 24.2 us
    add x4 -> x3, other arithmetic: 9.85 us -> 5.76 us  [prefix_states(): lax.associative_scan(join_states, (factor, update), axis=0)]
    pad x6, local copies, waits for them, and re-layouts: 52.3 us -> 56 us  [prefix_states(): lax.associative_scan(join_states, (factor, update), axis=0)]
    unnamed x19 -> x18, local copies, waits for them, and re-layouts: 12.9 us -> 13.5 us
  transfers between devices with their start and end apart: 3 -> 3, of which waited for: 2 -> 2; matrix products, arithmetic and copies ran while one was open for 13% -> 12% of each run, Pallas kernels for 0% -> 0%
where the time goes in v1:
time: 353 us; the launch traced here: 350 us
  waiting for transfers between devices  157 us (44%)
  local copies, waits for them, and re-layouts  89.3 us (25%)
  other arithmetic  51.6 us (15%)
  matrix products  32.2 us (9%)
  starting transfers between devices  17.4 us (5%)
    all_to_all x1, waiting for transfers between devices, shards(): lax.all_to_all(device_update.reshape(1, HEADS, HEAD_DIM, HEAD_DIM), 'seq'...  90.1 us
    all_to_all x1, waiting for transfers between devices, supply_map(): row_out = jax.lax.all_to_all(fresh, 'seq', 0, 0)  67.1 us
    pad x6, local copies, waits for them, and re-layouts, prefix_states(): lax.associative_scan(join_states, (factor, update), axis=0)  56 us
    unnamed x14, other arithmetic  24.2 us
    dot_general x1, matrix products, with_state(): jnp.einsum('nihd,nhde->nihe', query_rows.astype(jnp.float32), states, pre...  13.6 us
    unnamed x18, local copies, waits for them, and re-layouts  13.5 us
    dot_general x1, matrix products, local_terms(): jnp.einsum('ghij,gjhd->gihd', weights, value_blk, preferred_element_type=...  11.7 us
    reshape x1, local copies, waits for them, and re-layouts, shards(): with_state(query_rows, inside, leading, states)  8.91 us
  transfers between devices with their start and end apart: 3, of which 2 were waited for; matrix products, arithmetic and copies ran while one was open for 12% of the time, Pallas kernels for 0%

profile of v1, /device:TPU:13, one launch (start us, length us, event | category | flops | bytes accessed | tf_op | source)
XLA Modules:
  0.0 349.8 jit_solution(724919590423064499)
XLA Ops:
  0.7 0.8 reduce-window.8
  1.6 0.7 slice.159
  2.2 0.5 slice.162
  4.0 0.2 fusion.40
  4.2 0.2 multiply_reduce_fusion.1
  4.4 0.7 mul.191
  5.1 6.5 %all-to-all-start.1 = ((f32[1,16,4]{2,0,1:T(1,128)}), f32[1,16,4]{2,0,1:T(1,128)S(1)}, u32[]{:S(2)}, u32[]{:S(2)}) async-start(f32[1,16,4]{2,0,1:T(1,128)} %bitcast.18), calls=%async_computation.1 | async-start | bytes 16384 | tf_op jit(solution)/shard_map/all_to_all | solution.py:109
  11.6 6.4 %copy.65 = bf16[256,8192]{0,1:T(8,128)(2,1)} copy(bf16[256,8192]{1,0:T(8,128)(2,1)} %param.8) | data formatting | bytes 8388608 | tf_op jit(solution)/shard_map/reshape.12
  18.0 1.2 compare_convert_fusion.1
  19.3 6.7 %fusion.17 = f32[1,64,128,128]{3,2,0,1:T(8,128)} fusion(bf16[256,64,128]{0,2,1:T(8,128)(2,1)} %bitcast.145, f32[256,64]{0,1:T(8,128)S(1)} %get-tuple-element.32, bf16[256,8192]{1,0:T(8,128)(2,1)} %param.9), kind=kOutput, calls=%fused_computation.18 | convolution fusion | flops 543162368 | bytes 12648448 | tf_op jit(solution)/shard_map/while/body/eval_jaxpr/gjhd,gjhe->ghde/dot_general | solution.py:40
  26.0 6.0 %all-to-all-start = ((f32[1,64,128,128]{3,2,0,1:T(8,128)}), f32[1,64,128,128]{3,2,0,1:T(8,128)}, u32[]{:S(2)}, u32[]{:S(2)}) async-start(f32[1,64,128,128]{3,2,0,1:T(8,128)} %fusion.17), calls=%async_computation | async-start | bytes 8388608 | tf_op jit(solution)/shard_map/all_to_all | solution.py:112
  32.1 0.7 broadcast_dynamic-update-slice_fusion
  32.9 0.1 slice.133
  33.0 0.1 slice.137
  33.1 0.1 slice.139
  33.4 0.1 slice.145
  33.7 0.1 slice.132
  34.1 0.2 slice_reduce_fusion.2
  34.3 0.2 slice_reduce_fusion.1
  34.5 90.1 %all-to-all-done = f32[1,64,128,128]{3,2,0,1:T(8,128)} async-done(((f32[1,64,128,128]{3,2,0,1:T(8,128)}), f32[1,64,128,128]{3,2,0,1:T(8,128)}, u32[]{:S(2)}, u32[]{:S(2)}) %all-to-all-start) | async-done | bytes 4194336 | tf_op jit(solution)/shard_map/all_to_all | solution.py:112
  124.5 2.5 slice_add_fusion
  127.0 0.2 slice_add_fusion.1
  127.2 0.1 slice_add_fusion.2
  127.4 0.8 pad_add_fusion
  128.3 0.1 fusion.43
  128.4 0.8 pad_maximum_fusion.2
  129.2 3.5 %pad.27 = f32[4,4,128,128]{3,2,1,0:T(8,128)S(1)} pad(f32[2,4,128,128]{3,2,1,0:T(8,128)} %pad_maximum_fusion.2, f32[]{:T(128)} %constant.28.clone.1), padding=0_1_1x0_0_0x0_0_0x0_0_0 | pad | bytes 1572868 | tf_op jit(solution)/shard_map/pad | solution.py:72
  132.7 5.7 %pad.28 = f32[4,4,128,128]{3,2,1,0:T(8,128)} pad(f32[2,4,128,128]{3,2,1,0:T(8,128)} %pad_add_fusion, f32[]{:T(128)} %constant.28.clone.1), padding=1_0_1x0_0_0x0_0_0x0_0_0 | pad | bytes 1572868 | tf_op jit(solution)/shard_map/pad | solution.py:72
  138.4 2.3 add.94
  140.8 10.1 %pad.30 = f32[8,4,128,128]{3,2,1,0:T(8,128)} pad(f32[4,4,128,128]{3,2,1,0:T(8,128)} %add.94, f32[]{:T(128)} %constant.28.clone.1), padding=1_0_1x0_0_0x0_0_0x0_0_0 | pad | bytes 3145732 | tf_op jit(solution)/shard_map/pad | solution.py:72
  150.9 1.3 fusion.21
  152.3 6.3 %pad.29 = f32[8,4,128,128]{3,2,1,0:T(8,128)} pad(f32[4,4,128,128]{3,2,1,0:T(8,128)S(1)} %pad_maximum_fusion.1, f32[]{:T(128)} %constant.28.clone.1), padding=0_1_1x0_0_0x0_0_0x0_0_0 | pad | bytes 3145732 | tf_op jit(solution)/shard_map/pad | solution.py:72
  158.6 2.6 add.96
  161.2 0.2 copy-done.2
  161.5 0.6 copy-done.3
  162.1 1.8 fusion.20
  163.9 1.0 slice_bitcast_fusion
  164.9 1.5 pad_maximum_fusion
  166.4 18.4 %pad.31 = f32[16,4,128,128]{3,2,1,0:T(8,128)} pad(f32[8,4,128,128]{3,2,1,0:T(8,128)} %pad_maximum_fusion, f32[]{:T(128)} %constant.28.clone.1), padding=0_1_1x0_0_0x0_0_0x0_0_0 | pad | bytes 6291460 | tf_op jit(solution)/shard_map/pad | solution.py:72
  184.8 12.0 %pad.32 = f32[16,4,128,128]{3,2,1,0:T(8,128)} pad(f32[8,4,128,128]{3,2,1,0:T(8,128)S(1)} %add.96, f32[]{:T(128)} %constant.28.clone.1), padding=1_0_1x0_0_0x0_0_0x0_0_0 | pad | bytes 6291460 | tf_op jit(solution)/shard_map/pad | solution.py:72
  196.8 1.9 fusion.39
  198.7 1.8 fusion.38
  200.4 1.8 fusion.37
  202.2 1.8 fusion.36
  203.9 1.8 fusion.35
  205.7 1.8 fusion.34
  207.5 1.7 fusion.33
  209.2 1.7 fusion.32
  210.8 1.7 fusion.31
  212.5 1.7 fusion.30
  214.2 1.7 fusion.29
  215.9 1.7 fusion.28
  217.6 1.7 fusion.27
  219.3 1.7 fusion.26
  221.0 1.7 fusion.25
  222.6 4.9 %all-to-all-start.2 = ((f32[16,1,4,128,128]{4,3,2,1,0:T(8,128)}), f32[16,1,4,128,128]{4,3,2,1,0:T(8,128)}, u32[]{:S(2)}, u32[]{:S(2)}) async-start(f32[16,1,4,128,128]{4,3,2,1,0:T(8,128)} %fusion.25), calls=%async_computation.2 | async-start | bytes 8388608 | tf_op jit(solution)/shard_map/all_to_all | solution.py:91
  227.6 0.1 fusion.41
  227.7 11.7 %fusion.2 = f32[64,256,128]{1,2,0:T(8,128)} fusion(bf16[256,64,128]{0,2,1:T(8,128)(2,1)} %bitcast.146, f32[64,256]{1,0:T(8,128)S(1)} %bitcast.148, pred[256,256]{1,0:T(8,128)(4,1)S(1)} %fusion.41, bf16[256,8192]{1,0:T(8,128)(2,1)} %param.9, bf16[256,8192]{1,0:T(8,128)(2,1)} %param.7), kind=kOutput, calls=%fused_computation.7 | convolution fusion | flops 2168455168 | bytes 21102592 | tf_op jit(solution)/shard_map/while/body/eval_jaxpr/ghij,gjhd->gihd/dot_general | solution.py:34
  239.4 11.9 %pad.61 = f32[15,4,128,128]{3,2,1,0:T(8,128)} pad(f32[8,4,128,128]{3,2,1,0:T(8,128)S(1)} %add.96, f32[]{:T(128)} %constant.28.clone.1), padding=0_0_1x0_0_0x0_0_0x0_0_0 | pad | bytes 6029316
  251.3 1.7 add_bitcast_fusion.15
  252.9 67.1 %all-to-all-done.2 = f32[16,1,4,128,128]{4,3,2,1,0:T(8,128)} async-done(((f32[16,1,4,128,128]{4,3,2,1,0:T(8,128)}), f32[16,1,4,128,128]{4,3,2,1,0:T(8,128)}, u32[]{:S(2)}, u32[]{:S(2)}) %all-to-all-start.2) | async-done | bytes 4194336 | tf_op jit(solution)/shard_map/all_to_all | solution.py:91
  320.0 13.6 %multiply_reduce_fusion = (f32[256]{0:T(256)S(1)}, f32[1,256,64,128]{1,3,2,0:T(8,128)}) fusion(f32[256,64]{0,1:T(8,128)S(1)} %get-tuple-element.44, f32[64,128,128]{2,1,0:T(8,128)} %bitcast.48, f32[64,256,128]{1,2,0:T(8,128)} %fusion.2, bf16[256,8192]{1,0:T(8,128)(2,1)} %param.7), kind=kOutput, calls=%fused_computation.4 | convolution fusion | flops 3229613824 | bytes 25232384 | tf_op jit(solution)/shard_map/nihd,nhde->nihe/dot_general | solution.py:79
  333.7 8.9 %copy.64 = f32[256,8192]{1,0:T(8,128)} copy(f32[256,8192]{0,1:T(8,128)} %bitcast.144) | data formatting | bytes 16777216 | tf_op jit(solution)/shard_map/reshape | solution.py:125
  342.6 7.2 %multiply_convert_fusion.1 = bf16[256,8192]{1,0:T(8,128)(2,1)} fusion(bf16[256,8192]{1,0:T(8,128)(2,1)} %param.11, f32[256,8192]{1,0:T(8,128)} %copy.64, f32[8192]{0:T(1024)S(1)} %copy-done.7, f32[256]{0:T(256)S(1)} %add_rsqrt_fusion), kind=kLoop, calls=%fused_computation.3 | loop fusion | flops 16777216 | bytes 16811008 | tf_op jit(solution)/shard_map/convert_element_type | solution.py:130
  (34 shorter events, 1.2 us)
Async XLA Ops:
  0.6 3.4 copy-start
  4.2 15.1 %copy-start.5 = (f32[256,64]{0,1:T(8,128)}, f32[256,64]{0,1:T(8,128)S(1)}, u32[]{:S(2)}) copy-start(f32[256,64]{0,1:T(8,128)S(1)} %fusion.40) | copy-start | bytes 196612
  5.1 20.9 %all-to-all-start.1 = ((f32[1,16,4]{2,0,1:T(1,128)}), f32[1,16,4]{2,0,1:T(1,128)S(1)}, u32[]{:S(2)}, u32[]{:S(2)}) async-start(f32[1,16,4]{2,0,1:T(1,128)} %bitcast.18), calls=%async_computation.1 | async-start | bytes 16384 | tf_op jit(solution)/shard_map/all_to_all | solution.py:109
  26.0 98.5 %all-to-all-start = ((f32[1,64,128,128]{3,2,0,1:T(8,128)}), f32[1,64,128,128]{3,2,0,1:T(8,128)}, u32[]{:S(2)}, u32[]{:S(2)}) async-start(f32[1,64,128,128]{3,2,0,1:T(8,128)} %fusion.17), calls=%async_computation | async-start | bytes 8388608 | tf_op jit(solution)/shard_map/all_to_all | solution.py:112
  158.6 2.9 copy-start.2
  158.6 3.5 copy-start.3
  196.7 10.7 %copy-start.4 = (f32[16,4,128,128]{3,2,1,0:T(8,128)S(1)}, f32[16,4,128,128]{3,2,1,0:T(8,128)}, u32[]{:S(2)}) copy-start(f32[16,4,128,128]{3,2,1,0:T(8,128)} %pad.31) | copy-start | bytes 12582916
  222.6 5.0 %copy-start.6 = (f32[256,64]{0,1:T(8,128)S(1)}, f32[256,64]{0,1:T(8,128)}, u32[]{:S(2)}) copy-start(f32[256,64]{0,1:T(8,128)} %copy-done.5) | copy-start | bytes 196612
  222.6 97.4 %all-to-all-start.2 = ((f32[16,1,4,128,128]{4,3,2,1,0:T(8,128)}), f32[16,1,4,128,128]{4,3,2,1,0:T(8,128)}, u32[]{:S(2)}, u32[]{:S(2)}) async-start(f32[16,1,4,128,128]{4,3,2,1,0:T(8,128)} %fusion.25), calls=%async_computation.2 | async-start | bytes 8388608 | tf_op jit(solution)/shard_map/all_to_all | solution.py:91
  333.7 8.9 %copy-start.7 = (f32[8192]{0:T(1024)S(1)}, f32[8192]{0:T(1024)}, u32[]{:S(2)}) copy-start(f32[8192]{0:T(1024)} %param.12) | copy-start | bytes 98308
  342.6 7.2 %copy-start.1 = (bf16[256,64]{0,1:T(8,128)(2,1)S(1)}, bf16[256,64]{0,1:T(8,128)(2,1)}, u32[]{:S(2)}) copy-start(bf16[256,64]{0,1:T(8,128)(2,1)} %param.10) | copy-start | bytes 98308
